TPU v7x, 32 devices: a whole 2x2x4 slice. The times are simulated.
32 devices in a mesh: dp: 16 (over z, y, x), fsdp: 2 (over core).
Axes of the slice: x: 2, y: 2, z: 4, core: 2. Of those that a mesh axis runs over, the one named last changes fastest.
Arguments:
- features: bfloat16 [64, 1128, 512], P(('dp', 'fsdp')), may hold values from -6 to 6
- cotangent: bfloat16 [64, 1128, 512], P(('dp', 'fsdp')), may hold values from -6 to 6
- counts: int32 [64], P(('dp', 'fsdp')), may hold values from 1 to 100, as said below
- weights: float32 [4096, 512], P(('dp', 'fsdp'))
- small_params: float32 [3584], replicated
- moments_old: float32 [2, 4096, 512], P(None, ('dp', 'fsdp')), as said below
- small_moments: float32 [2, 3584], replicated, as said below
- basis_attn: float32 [4, 512, 512], replicated, as said below
- basis_ffn: float32 [2, 1024, 1024], replicated, as said below
- basis_cols: float32 [6, 512, 512], replicated, as said below
Outputs:
- output: bfloat16 [64, 1128, 512], P(('dp', 'fsdp'))
- grad_input: float32 [64, 1128, 512], P(('dp', 'fsdp'))
- grad_weights: float32 [4096, 512], P(('dp', 'fsdp'))
- moments_new: float32 [2, 4096, 512], P(None, ('dp', 'fsdp'))
- weights_new: float32 [4096, 512], P(('dp', 'fsdp'))
- grad_small: float32 [3584], replicated
- small_moments_new: float32 [2, 3584], replicated
- small_new: float32 [3584], replicated
Inputs may be any that keep to these rules, and one draw needn't show every extreme that they name: `counts`: some neighbourhood has 100 live queries and some has 1. `basis_attn`: each of the four matrices is orthogonal. `basis_ffn`: each of the two matrices is orthogonal. `basis_cols`: each of the six matrices is orthogonal. `moments_old`: second moments (index 1) are positive. `small_moments`: second moments (index 1) are positive.
All inputs are finite; a program needn't handle non-finite values.
Results may differ from a plain program's by a relative error of at most 0.014.
The roundings to bfloat16 on the way count: a program that leaves them out, or rounds other values in their place, can miss the bound.
Values may be sent and summed in bfloat16 or wider, within the bound.
No kernel may reach another device: no remote copies, remote signals or barrier semaphores. Data moves between devices by JAX's collectives and lax.ppermute only.
A program may use at most 320 MiB of HBM per device.

v0:
```python
import jax
import jax.numpy as jnp
from jax import lax
from jax.sharding import PartitionSpec as P

D = 512
HEADS = 4
FF = 1024
HD = 128
CTX = 1024
QCAP = 104
STEP = 10
SLOTS = 1128
MROWS = 4096
SMALL = 3584


eps_norm = 1e-05
eps_adam = 1e-08
beta_one = 0.9
beta_two = 0.999
rate_mats = 0.1
rate_small = 0.5
highest = lax.Precision.HIGHEST


def to_plain(stacked):
    width = stacked.shape[1]
    groups = stacked.reshape(D, 8, width)
    return jnp.concatenate(
        [
            groups[:, 0],
            groups[:, 1],
            groups[:, 2],
            groups[:, 3],
            groups[:, 4:6].reshape(FF, width),
            groups[:, 6:8].reshape(FF, width),
        ],
        axis=0,
    )


def to_stacked(plain):
    width = plain.shape[1]
    attn = jnp.transpose(plain[0 : 4 * D].reshape(4, D, width), (1, 0, 2))
    inner = plain[4 * D : 4 * D + FF].reshape(D, 2, width)
    outer = plain[4 * D + FF : 4 * D + 2 * FF].reshape(D, 2, width)
    return jnp.concatenate([attn, inner, outer], axis=1).reshape(MROWS, width)


def layer_norm(values, gain_vec, shift_vec):
    center = values - jnp.mean(values, axis=-1, keepdims=True)
    spread = jnp.mean(center * center, axis=-1, keepdims=True)
    return center * lax.rsqrt(spread + eps_norm) * gain_vec + shift_vec


def gelu_exact(values):
    return 0.5 * values * (1.0 + lax.erf(values * 0.7071067811865476))


def times_t(first_mat, second_mat):
    return lax.dot_general(
        first_mat, second_mat, (((1,), (1,)), ((), ())), preferred_element_type=jnp.float32
    )


def outer_sum(first_mat, second_mat):
    return lax.dot_general(
        first_mat, second_mat, (((0,), (0,)), ((), ())), preferred_element_type=jnp.float32
    )


def split_small(small_params):
    return (
        small_params[0:D],
        small_params[D : 2 * D],
        small_params[2 * D : 2 * D + FF],
        small_params[2 * D + FF : 3 * D + FF],
        small_params[3 * D + FF : 4 * D + FF],
        small_params[4 * D + FF : 5 * D + FF],
    )


def split_weights(plain_w):
    return (
        plain_w[0:D],
        plain_w[D : 2 * D],
        plain_w[2 * D : 3 * D],
        plain_w[3 * D : 4 * D],
        plain_w[4 * D : 4 * D + FF],
        plain_w[4 * D + FF : 4 * D + 2 * FF],
    )


def hood_forward(rows_in, live_rows, plain_w, small_params):
    scaling = HD ** (-0.5)
    w_query, w_key, w_value, w_output, w_hidden, w_back = split_weights(plain_w)
    gain_one, shift_one, bias_hidden, bias_output, gain_two, shift_two = split_small(small_params)
    context = rows_in[0:CTX]
    queries = (times_t(rows_in, w_query) * scaling).astype(jnp.bfloat16).reshape(SLOTS, HEADS, HD)
    key_rows = times_t(context, w_key).astype(jnp.bfloat16).reshape(CTX, HEADS, HD)
    value_rows = times_t(context, w_value).astype(jnp.bfloat16).reshape(CTX, HEADS, HD)
    scores = jnp.einsum("shd,chd->hsc", queries, key_rows, preferred_element_type=jnp.float32)
    row_top = jnp.max(scores, axis=-1, keepdims=True)
    exponent = jnp.exp(scores - row_top)
    sum_exp = jnp.sum(exponent, axis=-1, keepdims=True)
    soft_weights = exponent / sum_exp
    log_total = row_top + jnp.log(sum_exp)
    mixture = (
        jnp.einsum(
            "hsc,chd->shd",
            soft_weights.astype(jnp.bfloat16),
            value_rows,
            preferred_element_type=jnp.float32,
        )
        .reshape(SLOTS, D)
        .astype(jnp.bfloat16)
    )
    first_sum = rows_in.astype(jnp.float32) + times_t(mixture, w_output)
    normed = layer_norm(first_sum, gain_one, shift_one)
    hidden = times_t(normed.astype(jnp.bfloat16), w_hidden) + bias_hidden
    activated = gelu_exact(hidden).astype(jnp.bfloat16)
    second_sum = (
        normed + jnp.dot(activated, w_back, preferred_element_type=jnp.float32) + bias_output
    )
    output = (layer_norm(second_sum, gain_two, shift_two) * live_rows[:, None]).astype(jnp.bfloat16)
    return (
        output,
        (
            queries,
            key_rows,
            value_rows,
            log_total,
            mixture,
            first_sum,
            normed,
            hidden,
            activated,
            second_sum,
        ),
    )


def hood_backward(rows_in, live_rows, back_rows, kept_one, plain_w, small_params):
    (
        queries,
        key_rows,
        value_rows,
        log_total,
        mixture,
        first_sum,
        normed,
        hidden,
        activated,
        second_sum,
    ) = kept_one
    scaling = HD ** (-0.5)
    w_query, w_key, w_value, w_output, w_hidden, w_back = split_weights(plain_w)
    gain_one, shift_one, bias_hidden, bias_output, gain_two, shift_two = split_small(small_params)
    back_out = back_rows.astype(jnp.float32) * live_rows[:, None]
    ignored, pull_two = jax.vjp(layer_norm, second_sum, gain_two, shift_two)
    d_second, d_gain_two, d_shift_two = pull_two(back_out)
    d_branch = d_second.astype(jnp.bfloat16)
    d_bias_output = jnp.sum(d_branch.astype(jnp.float32), axis=0)
    grad_back = outer_sum(activated, d_branch)
    d_activated = times_t(d_branch, w_back)
    ignored, pull_gelu = jax.vjp(gelu_exact, hidden)
    d_hidden = pull_gelu(d_activated)[0].astype(jnp.bfloat16)
    d_bias_hidden = jnp.sum(d_hidden.astype(jnp.float32), axis=0)
    grad_hidden = outer_sum(d_hidden, normed.astype(jnp.bfloat16))
    d_normed = d_second + jnp.dot(d_hidden, w_hidden, preferred_element_type=jnp.float32)
    ignored, pull_one = jax.vjp(layer_norm, first_sum, gain_one, shift_one)
    d_first, d_gain_one, d_shift_one = pull_one(d_normed)
    d_attended = d_first.astype(jnp.bfloat16)
    grad_output = outer_sum(d_attended, mixture)
    d_mixture = (
        jnp.dot(d_attended, w_output, preferred_element_type=jnp.float32)
        .astype(jnp.bfloat16)
        .reshape(SLOTS, HEADS, HD)
    )
    scores = jnp.einsum("shd,chd->hsc", queries, key_rows, preferred_element_type=jnp.float32)
    soft_weights = jnp.exp(scores - log_total)
    d_soft = jnp.einsum("shd,chd->hsc", d_mixture, value_rows, preferred_element_type=jnp.float32)
    inner_sum = jnp.sum(soft_weights * d_soft, axis=-1, keepdims=True)
    d_scores = (soft_weights * (d_soft - inner_sum)).astype(jnp.bfloat16)
    d_values = (
        jnp.einsum(
            "hsc,shd->chd",
            soft_weights.astype(jnp.bfloat16),
            d_mixture,
            preferred_element_type=jnp.float32,
        )
        .astype(jnp.bfloat16)
        .reshape(CTX, D)
    )
    d_queries = (
        jnp.einsum("hsc,chd->shd", d_scores, key_rows, preferred_element_type=jnp.float32)
        .astype(jnp.bfloat16)
        .reshape(SLOTS, D)
    )
    d_keys = (
        jnp.einsum("hsc,shd->chd", d_scores, queries, preferred_element_type=jnp.float32)
        .astype(jnp.bfloat16)
        .reshape(CTX, D)
    )
    context = rows_in[0:CTX]
    grad_query = outer_sum(d_queries, rows_in) * scaling
    grad_key = outer_sum(d_keys, context)
    grad_value = outer_sum(d_values, context)
    d_context = jnp.dot(d_keys, w_key, preferred_element_type=jnp.float32) + jnp.dot(
        d_values, w_value, preferred_element_type=jnp.float32
    )
    d_rows = (
        d_first
        + jnp.dot(d_queries, w_query, preferred_element_type=jnp.float32) * scaling
        + jnp.concatenate([d_context, jnp.zeros((QCAP, D), jnp.float32)], axis=0)
    )
    grads_w = to_stacked(
        jnp.concatenate(
            [grad_query, grad_key, grad_value, grad_output, grad_hidden, grad_back], axis=0
        )
    )
    grads_s = jnp.concatenate(
        [d_gain_one, d_shift_one, d_bias_hidden, d_bias_output, d_gain_two, d_shift_two]
    )
    return (grads_w, grads_s, d_rows)


def row_vectors(block_ids, attn_vecs, ffn_vecs):
    pieces = []
    for slot_number in range(4):
        pieces.append(jnp.where((block_ids == slot_number)[:, None], attn_vecs, 0.0))
    for slot_number in range(2):
        pieces.append(jnp.where((block_ids == 4 + slot_number)[:, None], ffn_vecs, 0.0))
    return jnp.concatenate(pieces, axis=1)


def select_right(left_done, block_ids, basis_cols, transposed):
    if transposed:
        every = jnp.einsum("rk,blk->brl", left_done, basis_cols, precision=highest)
    else:
        every = jnp.einsum("rk,bkl->brl", left_done, basis_cols, precision=highest)
    onehot = (block_ids[None, :] == jnp.arange(6, dtype=jnp.int32)[:, None]).astype(jnp.float32)
    return jnp.sum(onehot[:, :, None] * every, axis=0)


def adam_step(grad, moments):
    first_new = beta_one * moments[0] + (1.0 - beta_one) * grad
    second_new = beta_two * moments[1] + (1.0 - beta_two) * grad * grad
    direction = (
        first_new
        / (1.0 - beta_one**STEP)
        / (jnp.sqrt(second_new / (1.0 - beta_two**STEP)) + eps_adam)
    )
    return (jnp.stack([first_new, second_new]), direction)


def on_device(
    features,
    cotangent,
    counts,
    weights,
    small_params,
    moments_old,
    small_moments,
    basis_attn,
    basis_ffn,
    basis_cols,
):
    gathered = to_plain(
        lax.all_gather(weights.astype(jnp.bfloat16), ("dp", "fsdp"), axis=0, tiled=True)
    )
    slot_ids = jnp.arange(QCAP, dtype=jnp.int32)
    live_query = (slot_ids[None, :] < counts[:, None]).astype(jnp.float32)
    live_all = jnp.concatenate([jnp.ones((counts.shape[0], CTX), jnp.float32), live_query], axis=1)

    def forward_one(packed):
        return hood_forward(packed[0], packed[1], gathered, small_params)

    output, kept = lax.map(forward_one, (features, live_all))
    back_weights = to_plain(
        lax.all_gather(weights.astype(jnp.bfloat16), ("dp", "fsdp"), axis=0, tiled=True)
    )

    def backward_one(totals, packed):
        rows_in, live_rows, back_rows, kept_one = packed
        grads_w, grads_s, d_rows = hood_backward(
            rows_in, live_rows, back_rows, kept_one, back_weights, small_params
        )
        return ((totals[0] + grads_w, totals[1] + grads_s), d_rows)

    initial = (jnp.zeros((MROWS, D), jnp.float32), jnp.zeros((SMALL,), jnp.float32))
    (sum_weights, sum_small), grad_input = lax.scan(
        backward_one, initial, (features, live_all, cotangent, kept)
    )
    grad_weights = lax.psum_scatter(sum_weights, ("dp", "fsdp"), scatter_dimension=0, tiled=True)
    grad_small = lax.psum(sum_small, ("dp", "fsdp"))
    count_rows = grad_weights.shape[0]
    row_ids = lax.axis_index(("dp", "fsdp")) * count_rows + jnp.arange(count_rows, dtype=jnp.int32)
    within = row_ids % 8
    group_ids = row_ids // 8
    block_ids = jnp.where(within < 4, within, 4 + (within - 4) // 2)
    inner_ids = jnp.where(within < 4, group_ids, 2 * group_ids + within % 2)
    attn_pick = jnp.minimum(block_ids, 3)
    ffn_pick = jnp.clip(block_ids - 4, 0, 1)
    attn_inner = jnp.minimum(inner_ids, D - 1)
    full_grad = to_plain(
        lax.all_gather(
            grad_weights.astype(jnp.bfloat16), ("dp", "fsdp"), axis=0, tiled=True
        ).astype(grad_weights.dtype)
    )
    left_fwd = row_vectors(
        block_ids, basis_attn[attn_pick, :, attn_inner], basis_ffn[ffn_pick, :, inner_ids]
    )
    rotated = select_right(
        jnp.dot(left_fwd, full_grad, precision=highest), block_ids, basis_cols, False
    )
    moments_new, direction = adam_step(rotated, moments_old)
    full_direction = to_plain(
        lax.all_gather(direction.astype(jnp.bfloat16), ("dp", "fsdp"), axis=0, tiled=True).astype(
            direction.dtype
        )
    )
    left_back = row_vectors(
        block_ids, basis_attn[attn_pick, attn_inner, :], basis_ffn[ffn_pick, inner_ids, :]
    )
    update = select_right(
        jnp.dot(left_back, full_direction, precision=highest), block_ids, basis_cols, True
    )
    weights_new = weights - rate_mats * update
    small_moments_new, small_direction = adam_step(grad_small, small_moments)
    small_new = small_params - rate_small * small_direction
    return (
        output,
        grad_input,
        grad_weights,
        moments_new,
        weights_new,
        grad_small,
        small_moments_new,
        small_new,
    )


def solution(mesh):
    placed = (
        P(("dp", "fsdp"), None, None),
        P(("dp", "fsdp"), None, None),
        P(("dp", "fsdp")),
        P(("dp", "fsdp"), None),
        P(),
        P(None, ("dp", "fsdp"), None),
        P(),
        P(),
        P(),
        P(),
    )
    return jax.shard_map(
        on_device,
        mesh=mesh,
        in_specs=placed,
        out_specs=(
            P(("dp", "fsdp"), None, None),
            P(("dp", "fsdp"), None, None),
            P(("dp", "fsdp"), None),
            P(None, ("dp", "fsdp"), None),
            P(("dp", "fsdp"), None),
            P(),
            P(),
            P(),
        ),
        check_vma=False,
    )
```

profile of v0, /device:TPU:0, one launch (start us, length us, event | category | flops | bytes accessed | tf_op | source)
XLA Modules:
  0.0 938.2 jit_solution(14671218755652624623)
XLA Ops:
  11.9 64.3 %all-gather.4.cloned.1.call-done = bf16[4096,512]{1,0:T(8,128)(2,1)} async-done(((bf16[128,512]{1,0:T(8,128)(2,1)}), bf16[4096,512]{1,0:T(8,128)(2,1)}) %all-gather.4.cloned.1.call-update) | async-done | bytes 4194320 | tf_op jit(solution)/shard_map/all_gather | solution.py:271
  76.2 10.9 %fusion.135 = (bf16[512,1,512]{2,1,0:T(2,128)(2,1)}, bf16[512,1,512]{2,1,0:T(2,128)(2,1)}, bf16[512,1,512]{2,1,0:T(2,128)(2,1)S(1)}, bf16[512,1,512]{2,1,0:T(2,128)(2,1)}) fusion(bf16[512,8,512]{2,1,0:T(8,128)(2,1)} %bitcast.440), kind=kLoop, calls=%fused_computation.301 | loop fusion | bytes 4194304 | tf_op jit(solution)/shard_map/slice | solution.py:35
  101.0 132.9 %while.45 = (s32[]{:T(128)}, bf16[2,1128,512]{2,1,0:T(8,128)(2,1)}, bf16[2,1128,4,128]{3,2,1,0:T(4,128)(2,1)}, bf16[2,1024,4,128]{1,3,2,0:T(8,128)(2,1)}, bf16[2...) while((s32[]{:T(128)}, bf16[2,1128,512]{2,1,0:T(8,128)(2,1)}, ...), condition=%wide.region_7.8_spmd, body=%wide.region_0.7_spmd.sunk | while | flops 7043044864 | bytes 361587008 | solution.py:280
  106.0 8.9 fusion.248
  114.9 9.2 fusion.249
  127.3 8.7 fusion.250
  172.3 8.9 fusion.248
  181.3 9.2 fusion.249
  236.7 324.5 %while.46 = (s32[]{:T(128)}, f32[4096,512]{1,0:T(8,128)}, f32[3584]{0:T(1024)S(1)}, f32[2,1128,512]{2,1,0:T(8,128)}, bf16[2,1024,4,128]{1,3,2,0:T(8,128)(2,1)}, ...) while((s32[]{:T(128)}, f32[4096,512]{1,0:T(8,128)}, ...), condition=%wide.region_24.25_spmd.clone, body=%wide.region_8.24_spmd.clone.sunk | while | flops 15261694976 | bytes 625410112 | solution.py:293
  288.6 10.6 %fusion.290 = f32[4,1128,1024]{2,1,0:T(8,128)} fusion(bf16[2,1024,4,128]{1,3,2,0:T(8,128)(2,1)} %get-tuple-element.1114, s32[]{:T(128)} %get-tuple-element.1072, bf16[141,4,8,128]{3,2,1,0:T(8,128)(2,1)S(1)} %fusion.289), kind=kOutput, calls=%fused_computation.121.clone.1 | convolution fusion | flops 1182793728 | bytes 20685312 | tf_op jit(solution)/shard_map/while/body/eval_jaxpr/shd,chd->hsc/dot_general | solution.py:183
  300.8 12.0 %multiply_reduce_fusion.18 = (f32[4,1128]{1,0:T(4,128)S(1)}, f32[4,1128,1024]{2,1,0:T(8,128)}) fusion(f32[4,1128,1024]{2,1,0:T(8,128)} %fusion.290, f32[4,1128]{1,0:T(4,128)S(1)} %dynamic-slice_bitcast_fusion.16, bf16[2,1024,4,128]{1,3,2,0:T(8,128)(2,1)S(1)} %copy-done.20, s32[]{:T(128)} %get-tuple-element.1072, ...), kind=kOutput, calls=%fused_computation.56.clone.1 | convolution fusion | flops 1196650112 | bytes 39202436 | tf_op jit(solution)/shard_map/while/body/eval_jaxpr/shd,chd->hsc/dot_general | solution.py:181
  312.8 12.8 %multiply_convert_fusion.5 = bf16[4,1128,1024]{2,1,0:T(8,128)(2,1)S(1)} fusion(f32[4,1128,1024]{2,1,0:T(8,128)} %get-tuple-element.973, f32[4,1128,1024]{2,1,0:T(8,128)} %fusion.290, f32[4,1128]{1,0:T(4,128)S(1)} %get-tuple-element.974), kind=kLoop, calls=%fused_computation.55.clone.1 | loop fusion | flops 13860864 | bytes 46220928 | tf_op jit(solution)/shard_map/while/body/eval_jaxpr/convert_element_type | solution.py:185
  391.3 12.6 %bitcast_add_fusion.3 = f32[4096,512]{1,0:T(8,128)} fusion(f32[512,8,512]{2,0,1:T(8,128)} %pad_maximum_fusion.7, f32[4096,512]{1,0:T(8,128)} %get-tuple-element.1073, pred[]{:T(512)S(6)} %compare.100), kind=kLoop, calls=%fused_computation.61.clone.1 | loop fusion | flops 4194304 | bytes 25165824 | tf_op jit(solution)/shard_map/while/body/eval_jaxpr/add | solution.py:290
  434.3 10.6 %fusion.290 = f32[4,1128,1024]{2,1,0:T(8,128)} fusion(bf16[2,1024,4,128]{1,3,2,0:T(8,128)(2,1)} %get-tuple-element.1114, s32[]{:T(128)} %get-tuple-element.1072, bf16[141,4,8,128]{3,2,1,0:T(8,128)(2,1)S(1)} %fusion.289), kind=kOutput, calls=%fused_computation.121.clone.1 | convolution fusion | flops 1182793728 | bytes 20685312 | tf_op jit(solution)/shard_map/while/body/eval_jaxpr/shd,chd->hsc/dot_general | solution.py:183
  446.5 12.0 %multiply_reduce_fusion.18 = (f32[4,1128]{1,0:T(4,128)S(1)}, f32[4,1128,1024]{2,1,0:T(8,128)}) fusion(f32[4,1128,1024]{2,1,0:T(8,128)} %fusion.290, f32[4,1128]{1,0:T(4,128)S(1)} %dynamic-slice_bitcast_fusion.16, bf16[2,1024,4,128]{1,3,2,0:T(8,128)(2,1)S(1)} %copy-done.20, s32[]{:T(128)} %get-tuple-element.1072, ...), kind=kOutput, calls=%fused_computation.56.clone.1 | convolution fusion | flops 1196650112 | bytes 39202436 | tf_op jit(solution)/shard_map/while/body/eval_jaxpr/shd,chd->hsc/dot_general | solution.py:181
  458.5 12.8 %multiply_convert_fusion.5 = bf16[4,1128,1024]{2,1,0:T(8,128)(2,1)S(1)} fusion(f32[4,1128,1024]{2,1,0:T(8,128)} %get-tuple-element.973, f32[4,1128,1024]{2,1,0:T(8,128)} %fusion.290, f32[4,1128]{1,0:T(4,128)S(1)} %get-tuple-element.974), kind=kLoop, calls=%fused_computation.55.clone.1 | loop fusion | flops 13860864 | bytes 46220928 | tf_op jit(solution)/shard_map/while/body/eval_jaxpr/convert_element_type | solution.py:185
  536.9 15.0 %bitcast_add_fusion.3 = f32[4096,512]{1,0:T(8,128)} fusion(f32[512,8,512]{2,0,1:T(8,128)} %pad_maximum_fusion.7, f32[4096,512]{1,0:T(8,128)} %get-tuple-element.1073, pred[]{:T(512)S(6)} %compare.100), kind=kLoop, calls=%fused_computation.61.clone.1 | loop fusion | flops 4194304 | bytes 25165824 | tf_op jit(solution)/shard_map/while/body/eval_jaxpr/add | solution.py:290
  561.2 147.4 %reduce-scatter.2.cloned.1.call-done = f32[128,512]{1,0:T(8,128)} async-done(((f32[4096,512]{1,0:T(8,128)}), f32[128,512]{1,0:T(8,128)}) %reduce-scatter.2.cloned.1.call-update) | async-done | bytes 262160 | tf_op jit(solution)/shard_map/reduce_scatter | solution.py:296
  719.8 8.8 copy.69
  739.3 30.7 %all-gather.6.cloned.1.call-done = bf16[4096,512]{1,0:T(8,128)(2,1)} async-done(((bf16[128,512]{1,0:T(8,128)(2,1)}), bf16[4096,512]{1,0:T(8,128)(2,1)}) %all-gather.6.cloned.1.call-update) | async-done | bytes 4194320 | tf_op jit(solution)/shard_map/all_gather | solution.py:308
  780.6 10.1 %fusion.132 = (f32[512,2,512]{2,1,0:T(2,128)}, f32[512,2,512]{2,1,0:T(2,128)}) fusion(f32[512,8,512]{2,1,0:T(8,128)} %copy-done.23), kind=kLoop, calls=%fused_computation.298 | loop fusion | bytes 8388608 | tf_op jit(solution)/shard_map/slice | solution.py:37
  818.9 39.3 %psum.7 = f32[3584]{0:T(1024)S(1)} all-reduce(f32[3584]{0:T(1024)S(1)} %get-tuple-element.262), channel_id=1, replica_groups=mesh['dp'=16,'fsdp'=2] {'dp','fsdp'}, use_global_device_ids=true, to_apply=%region_28.29 | all-reduce | flops 3584 | bytes 28672 | tf_op jit(solution)/shard_map/psum | solution.py:297
  861.2 18.4 %all-gather.8.cloned.1.call-done = bf16[4096,512]{1,0:T(8,128)(2,1)} async-done(((bf16[128,512]{1,0:T(8,128)(2,1)}), bf16[4096,512]{1,0:T(8,128)(2,1)}) %all-gather.8.cloned.1.call-update) | async-done | bytes 4194320 | tf_op jit(solution)/shard_map/all_gather | solution.py:320
  890.1 10.1 %fusion.130 = (f32[512,2,512]{2,1,0:T(2,128)}, f32[512,2,512]{2,1,0:T(2,128)}) fusion(f32[512,8,512]{2,1,0:T(8,128)} %copy-done.24), kind=kLoop, calls=%fused_computation.296 | loop fusion | bytes 8388608 | tf_op jit(solution)/shard_map/slice | solution.py:37
  (508 shorter events, 407.9 us)
Async XLA Ops:
  7.2 69.0 %all-gather.4.cloned.1.call-start = ((), (), s32[]{:S(2)}) async-start(), calls=%async_computation.1 | async-start | bytes 4325376 | tf_op jit(solution)/shard_map/all_gather | solution.py:271
  8.9 699.8 %reduce-scatter.2.cloned.1.call-start = ((), (), s32[]{:S(2)}) async-start(), calls=%async_computation.2 | async-start | bytes 8650752 | tf_op jit(solution)/shard_map/reduce_scatter | solution.py:296
  76.2 10.9 %copy-start.29 = (bf16[4096,512]{1,0:T(8,128)(2,1)S(1)}, bf16[4096,512]{1,0:T(8,128)(2,1)}, u32[]{:S(2)}) copy-start(bf16[4096,512]{1,0:T(8,128)(2,1)} %all-gather.4.cloned.1.call-done) | copy-start | bytes 12582916
  103.5 11.5 %copy-start.9 = (bf16[1128,512]{1,0:T(8,128)(2,1)}, bf16[1128,512]{1,0:T(8,128)(2,1)S(1)}, u32[]{:S(2)}) copy-start(bf16[1128,512]{1,0:T(8,128)(2,1)S(1)} %fusion.247) | copy-start | bytes 3465220 | tf_op jit(solution)/shard_map/while
  169.8 11.5 %copy-start.9 = (bf16[1128,512]{1,0:T(8,128)(2,1)}, bf16[1128,512]{1,0:T(8,128)(2,1)S(1)}, u32[]{:S(2)}) copy-start(bf16[1128,512]{1,0:T(8,128)(2,1)S(1)} %fusion.247) | copy-start | bytes 3465220 | tf_op jit(solution)/shard_map/while
  312.8 21.3 %slice-start = ((s8[18481152]{0:T(1024)(128)(4,1)}), s8[4194304]{0:T(1024)(128)(4,1)S(1)}, s32[]{:S(2)}) async-start(s8[18481152]{0:T(1024)(128)(4,1)} %bitcast.409), calls=%async_computation.5 | async-start | bytes 8388608 | tf_op jit(solution)/shard_map/while
  312.8 21.3 %slice-start.1 = ((s8[18481152]{0:T(1024)(128)(4,1)}), s8[4194304]{0:T(1024)(128)(4,1)S(1)}, s32[]{:S(2)}) async-start(s8[18481152]{0:T(1024)(128)(4,1)} %bitcast.409), calls=%async_computation.6 | async-start | bytes 8388608 | tf_op jit(solution)/shard_map/while
  312.8 21.4 %slice-start.2 = ((s8[18481152]{0:T(1024)(128)(4,1)}), s8[4194304]{0:T(1024)(128)(4,1)S(1)}, s32[]{:S(2)}) async-start(s8[18481152]{0:T(1024)(128)(4,1)} %bitcast.409), calls=%async_computation.7 | async-start | bytes 8388608 | tf_op jit(solution)/shard_map/while
  312.8 21.4 %slice-start.3 = ((s8[18481152]{0:T(1024)(128)(4,1)}), s8[4194304]{0:T(1024)(128)(4,1)S(1)}, s32[]{:S(2)}) async-start(s8[18481152]{0:T(1024)(128)(4,1)} %bitcast.409), calls=%async_computation.8 | async-start | bytes 8388608 | tf_op jit(solution)/shard_map/while
  391.3 12.6 %copy-start.47 = (f32[512]{0:T(512)S(1)}, f32[512]{0:T(512)}, u32[]{:S(2)}) copy-start(f32[512]{0:T(512)} %get-tuple-element.975) | copy-start | bytes 6148 | tf_op jit(solution)/shard_map/while
  391.3 12.6 %copy-start.46 = (f32[512]{0:T(512)S(1)}, f32[512]{0:T(512)}, u32[]{:S(2)}) copy-start(f32[512]{0:T(512)} %get-tuple-element.976) | copy-start | bytes 6148 | tf_op jit(solution)/shard_map/while
  391.3 12.7 %copy-start.44 = (f32[1024]{0:T(1024)S(1)}, f32[1024]{0:T(1024)}, u32[]{:S(2)}) copy-start(f32[1024]{0:T(1024)} %get-tuple-element.977) | copy-start | bytes 12292 | tf_op jit(solution)/shard_map/while
  391.3 12.7 %copy-start.8 = (f32[1128,512]{1,0:T(8,128)S(1)}, f32[1128,512]{1,0:T(8,128)}, u32[]{:S(2)}) copy-start(f32[1128,512]{1,0:T(8,128)} %copy-done.7) | copy-start | bytes 6930436 | tf_op jit(solution)/shard_map/while
  458.4 21.3 %slice-start = ((s8[18481152]{0:T(1024)(128)(4,1)}), s8[4194304]{0:T(1024)(128)(4,1)S(1)}, s32[]{:S(2)}) async-start(s8[18481152]{0:T(1024)(128)(4,1)} %bitcast.409), calls=%async_computation.5 | async-start | bytes 8388608 | tf_op jit(solution)/shard_map/while
  458.4 21.3 %slice-start.1 = ((s8[18481152]{0:T(1024)(128)(4,1)}), s8[4194304]{0:T(1024)(128)(4,1)S(1)}, s32[]{:S(2)}) async-start(s8[18481152]{0:T(1024)(128)(4,1)} %bitcast.409), calls=%async_computation.6 | async-start | bytes 8388608 | tf_op jit(solution)/shard_map/while
  458.4 21.4 %slice-start.2 = ((s8[18481152]{0:T(1024)(128)(4,1)}), s8[4194304]{0:T(1024)(128)(4,1)S(1)}, s32[]{:S(2)}) async-start(s8[18481152]{0:T(1024)(128)(4,1)} %bitcast.409), calls=%async_computation.7 | async-start | bytes 8388608 | tf_op jit(solution)/shard_map/while
  458.5 21.4 %slice-start.3 = ((s8[18481152]{0:T(1024)(128)(4,1)}), s8[4194304]{0:T(1024)(128)(4,1)S(1)}, s32[]{:S(2)}) async-start(s8[18481152]{0:T(1024)(128)(4,1)} %bitcast.409), calls=%async_computation.8 | async-start | bytes 8388608 | tf_op jit(solution)/shard_map/while
  536.9 15.0 %copy-start.47 = (f32[512]{0:T(512)S(1)}, f32[512]{0:T(512)}, u32[]{:S(2)}) copy-start(f32[512]{0:T(512)} %get-tuple-element.975) | copy-start | bytes 6148 | tf_op jit(solution)/shard_map/while
  536.9 15.0 %copy-start.46 = (f32[512]{0:T(512)S(1)}, f32[512]{0:T(512)}, u32[]{:S(2)}) copy-start(f32[512]{0:T(512)} %get-tuple-element.976) | copy-start | bytes 6148 | tf_op jit(solution)/shard_map/while
  536.9 15.1 %copy-start.44 = (f32[1024]{0:T(1024)S(1)}, f32[1024]{0:T(1024)}, u32[]{:S(2)}) copy-start(f32[1024]{0:T(1024)} %get-tuple-element.977) | copy-start | bytes 12292 | tf_op jit(solution)/shard_map/while
  536.9 15.1 %copy-start.8 = (f32[1128,512]{1,0:T(8,128)S(1)}, f32[1128,512]{1,0:T(8,128)}, u32[]{:S(2)}) copy-start(f32[1128,512]{1,0:T(8,128)} %copy-done.7) | copy-start | bytes 6930436 | tf_op jit(solution)/shard_map/while
  561.2 208.9 %all-gather.6.cloned.1.call-start = ((), (), s32[]{:S(2)}) async-start(), calls=%async_computation.3 | async-start | bytes 4325376 | tf_op jit(solution)/shard_map/all_gather | solution.py:308
  710.3 169.2 %all-gather.8.cloned.1.call-start = ((), (), s32[]{:S(2)}) async-start(), calls=%async_computation.4 | async-start | bytes 4325376 | tf_op jit(solution)/shard_map/all_gather | solution.py:320
  858.2 24.7 %copy-start.45 = (f32[3584]{0:T(1024)}, f32[3584]{0:T(1024)S(1)}, u32[]{:S(2)}) copy-start(f32[3584]{0:T(1024)S(1)} %psum.7) | copy-start | bytes 43012
  (111 other events, 486.9 us)
Sparse Core Ops, SparseCore 0:
  11.4 64.7 all-gather.3
  561.3 147.2 reduce-scatter.1
  712.1 57.9 all-gather.5
  818.9 60.5 all-gather.7
where the time goes:
time: 945 us; the launch traced here: 938 us
  waiting for transfers between devices  261 us (28%)
  matrix products  245 us (26%)
  local copies, waits for them, and re-layouts  198 us (21%)
  other arithmetic  147 us (16%)
  blocking collectives  39.3 us (4%)
  loops' own time  32.5 us (3%)
  between operations  14.6 us (2%)
    reduce_scatter x1, waiting for transfers between devices, on_device(): lax.psum_scatter(sum_weights, ('dp', 'fsdp'), scatter_dimension=0, tiled=...  147 us
    all_gather x1, waiting for transfers between devices, on_device(): lax.all_gather(weights.astype(jnp.bfloat16), ('dp', 'fsdp'), axis=0, tile...  64.3 us
    unnamed x48, local copies, waits for them, and re-layouts  40.5 us
    psum x1, blocking collectives, on_device(): grad_small = lax.psum(sum_small, ('dp', 'fsdp'))  39.3 us
    dot_general x12, matrix products, times_t(): lax.dot_general(first_mat, second_mat, (((1,), (1,)), ((), ())), preferre...  37.3 us
    dot_general x12, matrix products, outer_sum(): lax.dot_general(first_mat, second_mat, (((0,), (0,)), ((), ())), preferre...  33.9 us
    while x238, local copies, waits for them, and re-layouts  32.5 us
    another operation x1, loops' own time, on_device(): lax.scan(backward_one, initial, (features, live_all, cotangent, kept))  31.7 us
  transfers between devices with their start and end apart: 4, of which 4 were waited for; matrix products, arithmetic and copies ran while one was open for 4% of the time, Pallas kernels for 0%

commit v1 on v0

v1 whole, which is shorter than its diff:
```python
import jax
import jax.numpy as jnp
from jax import lax
from jax.sharding import PartitionSpec as P
from jax.experimental import pallas as pl
from jax.experimental.pallas import tpu as pltpu

D = 512
HEADS = 4
FF = 1024
HD = 128
CTX = 1024
SLOTS = 1128
QCAP = 104
STEP = 10
MROWS = 4096
SMALL = 3584
PAD = 1152
RB = 384
NRB = PAD // RB
scaling = HD ** (-0.5)
eps_norm = 1e-05
eps_adam = 1e-08
beta_one = 0.9
beta_two = 0.999
rate_mats = 0.1
rate_small = 0.5
highest = lax.Precision.HIGHEST
bf16 = jnp.bfloat16
f32 = jnp.float32
VLIM = 58 * 1024 * 1024


def nt(a, b):
    return lax.dot_general(a, b, (((1,), (1,)), ((), ())), preferred_element_type=f32)


def nn(a, b):
    return lax.dot_general(a, b, (((1,), (0,)), ((), ())), preferred_element_type=f32)


def tn(a, b):
    return lax.dot_general(a, b, (((0,), (0,)), ((), ())), preferred_element_type=f32)


def attn_fwd_body(xc_ref, xr_ref, w_ref, q_ref, k_ref, v_ref, e_ref, o_ref, li_ref, ve_ref):
    rb = pl.program_id(1)

    @pl.when(rb == 0)
    def _():
        xc = xc_ref[0]
        k_ref[0] = nt(xc, w_ref[1]).astype(bf16)
        v_ref[0] = nt(xc, w_ref[2]).astype(bf16)
        for h in range(HEADS):
            ve_ref[h, :, 0:HD] = v_ref[0, :, h * HD : (h + 1) * HD]
            ve_ref[h, :, HD : 2 * HD] = jnp.ones((CTX, HD), bf16)

    rows = rb * RB + lax.broadcasted_iota(jnp.int32, (RB, 1), 0)
    xr = jnp.where(rows < SLOTS, xr_ref[0].astype(f32), 0.0).astype(bf16)
    q_ref[0] = (nt(xr, w_ref[0]) * scaling).astype(bf16)
    for h in range(HEADS):
        hs = slice(h * HD, (h + 1) * HD)
        s = nt(q_ref[0, :, hs], k_ref[0, :, hs])
        m = jnp.max(s, axis=-1, keepdims=True)
        e_ref[0, h] = jnp.exp(s - m).astype(bf16)
        ov = nn(e_ref[0, h], ve_ref[h])
        li = 1.0 / ov[:, HD:]
        li_ref[0, :, hs] = li
        o_ref[0, :, hs] = (ov[:, :HD] * li).astype(bf16)


def attn_fwd(x, wqkv):
    n = x.shape[0]
    sd = jax.ShapeDtypeStruct
    return pl.pallas_call(
        attn_fwd_body,
        grid=(n, NRB),
        in_specs=[
            pl.BlockSpec((1, CTX, D), lambda i, r: (i, 0, 0)),
            pl.BlockSpec((1, RB, D), lambda i, r: (i, r, 0)),
            pl.BlockSpec((3, D, D), lambda i, r: (0, 0, 0)),
        ],
        out_specs=[
            pl.BlockSpec((1, RB, D), lambda i, r: (i, r, 0)),
            pl.BlockSpec((1, CTX, D), lambda i, r: (i, 0, 0)),
            pl.BlockSpec((1, CTX, D), lambda i, r: (i, 0, 0)),
            pl.BlockSpec((1, HEADS, RB, CTX), lambda i, r: (i, 0, r, 0)),
            pl.BlockSpec((1, RB, D), lambda i, r: (i, r, 0)),
            pl.BlockSpec((1, RB, D), lambda i, r: (i, r, 0)),
        ],
        out_shape=[
            sd((n, PAD, D), bf16),
            sd((n, CTX, D), bf16),
            sd((n, CTX, D), bf16),
            sd((n, HEADS, PAD, CTX), bf16),
            sd((n, PAD, D), bf16),
            sd((n, PAD, D), f32),
        ],
        scratch_shapes=[pltpu.VMEM((HEADS, CTX, 2 * HD), bf16)],
        compiler_params=pltpu.CompilerParams(
            dimension_semantics=("arbitrary", "arbitrary"), vmem_limit_bytes=VLIM
        ),
        cost_estimate=pl.CostEstimate(
            flops=n * 14_000_000_000 // 2, transcendentals=n * HEADS * PAD * CTX, bytes_accessed=n * 20_000_000
        ),
        name="attention_forward",
    )(x, x, wqkv)


def lane_mean(v):
    return jnp.sum(v, axis=-1, keepdims=True) * (1.0 / D)


def rows_body(cnt_ref, x_ref, o_ref, li_ref, c_ref, wo_ref, wi_ref, wb_ref, sp_ref,
              out_ref, d1_ref, do_ref, go_ref, gi_ref, gb_ref, gs_ref):
    n, rb = pl.program_id(0), pl.program_id(1)
    first = jnp.logical_and(n == 0, rb == 0)

    @pl.when(first)
    def _():
        go_ref[...] = jnp.zeros_like(go_ref)
        gi_ref[...] = jnp.zeros_like(gi_ref)
        gb_ref[...] = jnp.zeros_like(gb_ref)
        gs_ref[...] = jnp.zeros_like(gs_ref)

    rows = rb * RB + lax.broadcasted_iota(jnp.int32, (RB, 1), 0)
    valid = rows < SLOTS
    live = rows < CTX + cnt_ref[n]
    gain1, shift1 = sp_ref[0:1], sp_ref[1:2]
    bias2, gain2, shift2 = sp_ref[4:5], sp_ref[5:6], sp_ref[6:7]
    bias1 = jnp.concatenate([sp_ref[2:3], sp_ref[3:4]], axis=1)
    o = o_ref[0]
    r1 = jnp.where(valid, x_ref[0].astype(f32), 0.0) + nt(o, wo_ref[...])
    c1 = r1 - lane_mean(r1)
    is1 = lax.rsqrt(lane_mean(c1 * c1) + eps_norm)
    xh1 = c1 * is1
    h = xh1 * gain1 + shift1
    hb = h.astype(bf16)
    u = nt(hb, wi_ref[...]) + bias1
    au = jnp.abs(u)
    ex = jnp.exp(-0.5 * u * u)
    t = 1.0 / (1.0 + 0.23164189 * au)
    poly = t * (0.127414796 + t * (-0.142248368 + t * (0.7107068705 + t * (-0.7265760135 + t * 0.5307027145))))
    tail = poly * ex
    phi = jnp.where(u >= 0.0, 1.0 - tail, tail)
    gb = (u * phi).astype(bf16)
    dgelu = phi + u * ex * 0.3989422804014327
    r2 = h + nn(gb, wb_ref[...]) + bias2
    c2 = r2 - lane_mean(r2)
    is2 = lax.rsqrt(lane_mean(c2 * c2) + eps_norm)
    xh2 = c2 * is2
    out_ref[0] = jnp.where(live, xh2 * gain2 + shift2, 0.0).astype(bf16)
    dy = jnp.where(live, c_ref[0].astype(f32), 0.0)
    gs_ref[5:6] += jnp.sum(dy * xh2, axis=0, keepdims=True)
    gs_ref[6:7] += jnp.sum(dy, axis=0, keepdims=True)
    e2 = dy * gain2
    d2 = (e2 - lane_mean(e2) - xh2 * lane_mean(e2 * xh2)) * is2
    df = d2.astype(bf16)
    gs_ref[4:5] += jnp.sum(df.astype(f32), axis=0, keepdims=True)
    gb_ref[...] += tn(gb, df)
    du = (nt(df, wb_ref[...]) * dgelu).astype(bf16)
    dub = jnp.sum(du.astype(f32), axis=0, keepdims=True)
    gs_ref[2:3] += dub[:, :D]
    gs_ref[3:4] += dub[:, D:]
    gi_ref[...] += tn(du, hb)
    dh = d2 + nn(du, wi_ref[...])
    gs_ref[0:1] += jnp.sum(dh * xh1, axis=0, keepdims=True)
    gs_ref[1:2] += jnp.sum(dh, axis=0, keepdims=True)
    e1 = dh * gain1
    d1 = (e1 - lane_mean(e1) - xh1 * lane_mean(e1 * xh1)) * is1
    d1_ref[0] = d1
    da = d1.astype(bf16)
    go_ref[...] += tn(da, o)
    do_ref[0] = (nn(da, wo_ref[...]) * li_ref[0]).astype(bf16)


def rows_pass(counts, x, o, li, cot, wo, wi, wb, sp):
    n = x.shape[0]
    sd = jax.ShapeDtypeStruct
    blk = pl.BlockSpec((1, RB, D), lambda i, r, c: (i, r, 0))
    const = lambda *s: pl.BlockSpec(s, lambda i, r, c: (0,) * len(s))
    return pl.pallas_call(
        rows_body,
        grid_spec=pltpu.PrefetchScalarGridSpec(
            num_scalar_prefetch=1,
            grid=(n, NRB),
            in_specs=[blk, blk, blk, blk, const(D, D), const(FF, D), const(FF, D), const(8, D)],
            out_specs=[blk, blk, blk, const(D, D), const(FF, D), const(FF, D), const(8, D)],
        ),
        out_shape=[
            sd((n, SLOTS, D), bf16),
            sd((n, PAD, D), f32),
            sd((n, PAD, D), bf16),
            sd((D, D), f32),
            sd((FF, D), f32),
            sd((FF, D), f32),
            sd((8, D), f32),
        ],
        compiler_params=pltpu.CompilerParams(
            dimension_semantics=("arbitrary", "arbitrary"), vmem_limit_bytes=VLIM
        ),
        cost_estimate=pl.CostEstimate(
            flops=n * 18_000_000_000 // 2, transcendentals=n * PAD * FF * 2, bytes_accessed=n * 15_000_000
        ),
        name="rows_forward_backward",
    )(counts, x, o, li, cot, wo, wi, wb, sp)


def attn_bwd_body(x_ref, q_ref, k_ref, v_ref, e_ref, o_ref, do_ref, acc_ref, w_ref,
                  gi_ref, gw_ref, dq_ref, dkt_ref, dvt_ref):
    n = pl.program_id(0)

    @pl.when(n == 0)
    def _():
        gw_ref[...] = jnp.zeros_like(gw_ref)

    for h in range(2):
        hs = slice(h * HD, (h + 1) * HD)
        dkt = jnp.zeros((HD, CTX), f32)
        dvt = jnp.zeros((HD, CTX), f32)
        for rb in range(NRB):
            rs = slice(rb * RB, (rb + 1) * RB)
            do = do_ref[0, rs, hs]
            dof = do.astype(f32)
            t = jnp.sum(dof * o_ref[0, rs, hs].astype(f32), axis=-1, keepdims=True)
            dp = nt(do, v_ref[0, :, hs])
            e = e_ref[0, h, rs]
            ds = (e.astype(f32) * (dp - t)).astype(bf16)
            dq_ref[rs, hs] = nn(ds, k_ref[0, :, hs]).astype(bf16)
            dvt = dvt + tn(do, e)
            dkt = dkt + tn(q_ref[0, rs, hs], ds)
        dkt_ref[hs] = dkt.astype(bf16)
        dvt_ref[hs] = dvt.astype(bf16)
    xc = x_ref[0, 0:CTX]
    gw_ref[0] += tn(dq_ref[0:CTX], xc) * scaling
    gw_ref[0] += tn(dq_ref[CTX:SLOTS], x_ref[0, CTX:SLOTS]) * scaling
    gw_ref[1] += nn(dkt_ref[...], xc)
    gw_ref[2] += nn(dvt_ref[...], xc)
    gi_ref[0, 0:CTX] = (
        acc_ref[0, 0:CTX]
        + nn(dq_ref[0:CTX], w_ref[0]) * scaling
        + tn(dkt_ref[...], w_ref[1])
        + tn(dvt_ref[...], w_ref[2])
    )
    gi_ref[0, CTX:SLOTS] = acc_ref[0, CTX:SLOTS] + nn(dq_ref[CTX:SLOTS], w_ref[0]) * scaling


def attn_bwd(pair, x, q, k, v, e, o, do, acc, wqkv):
    n = x.shape[0]
    sd = jax.ShapeDtypeStruct
    heads = lambda rows: pl.BlockSpec((1, rows, 2 * HD), lambda i: (i, 0, pair))
    return pl.pallas_call(
        attn_bwd_body,
        grid=(n,),
        in_specs=[
            pl.BlockSpec((1, SLOTS, D), lambda i: (i, 0, 0)),
            heads(PAD),
            heads(CTX),
            heads(CTX),
            pl.BlockSpec((1, 2, PAD, CTX), lambda i: (i, pair, 0, 0)),
            heads(PAD),
            heads(PAD),
            pl.BlockSpec((1, acc.shape[1], D), lambda i: (i, 0, 0)),
            pl.BlockSpec((3, 2 * HD, D), lambda i: (0, pair, 0)),
        ],
        out_specs=[
            pl.BlockSpec((1, SLOTS, D), lambda i: (i, 0, 0)),
            pl.BlockSpec((3, 2 * HD, D), lambda i: (0, 0, 0)),
        ],
        out_shape=[sd((n, SLOTS, D), f32), sd((3, 2 * HD, D), f32)],
        scratch_shapes=[
            pltpu.VMEM((PAD, 2 * HD), bf16),
            pltpu.VMEM((2 * HD, CTX), bf16),
            pltpu.VMEM((2 * HD, CTX), bf16),
        ],
        compiler_params=pltpu.CompilerParams(
            dimension_semantics=("arbitrary",), vmem_limit_bytes=VLIM
        ),
        cost_estimate=pl.CostEstimate(
            flops=n * 9_000_000_000 // 2, transcendentals=0, bytes_accessed=n * 12_000_000
        ),
        name="attention_backward",
    )(x, q, k, v, e, o, do, acc, wqkv)


def to_plain(stacked):
    width = stacked.shape[1]
    groups = stacked.reshape(D, 8, width)
    return jnp.concatenate(
        [
            groups[:, 0],
            groups[:, 1],
            groups[:, 2],
            groups[:, 3],
            groups[:, 4:6].reshape(FF, width),
            groups[:, 6:8].reshape(FF, width),
        ],
        axis=0,
    )


def to_stacked(plain):
    width = plain.shape[1]
    attn = jnp.transpose(plain[0 : 4 * D].reshape(4, D, width), (1, 0, 2))
    inner = plain[4 * D : 4 * D + FF].reshape(D, 2, width)
    outer = plain[4 * D + FF : 4 * D + 2 * FF].reshape(D, 2, width)
    return jnp.concatenate([attn, inner, outer], axis=1).reshape(MROWS, width)


def row_vectors(block_ids, attn_vecs, ffn_vecs):
    pieces = []
    for slot_number in range(4):
        pieces.append(jnp.where((block_ids == slot_number)[:, None], attn_vecs, 0.0))
    for slot_number in range(2):
        pieces.append(jnp.where((block_ids == 4 + slot_number)[:, None], ffn_vecs, 0.0))
    return jnp.concatenate(pieces, axis=1)


def select_right(left_done, block_ids, basis_cols, transposed):
    if transposed:
        every = jnp.einsum("rk,blk->brl", left_done, basis_cols, precision=highest)
    else:
        every = jnp.einsum("rk,bkl->brl", left_done, basis_cols, precision=highest)
    onehot = (block_ids[None, :] == jnp.arange(6, dtype=jnp.int32)[:, None]).astype(jnp.float32)
    return jnp.sum(onehot[:, :, None] * every, axis=0)


def adam_step(grad, moments):
    first_new = beta_one * moments[0] + (1.0 - beta_one) * grad
    second_new = beta_two * moments[1] + (1.0 - beta_two) * grad * grad
    direction = (
        first_new
        / (1.0 - beta_one**STEP)
        / (jnp.sqrt(second_new / (1.0 - beta_two**STEP)) + eps_adam)
    )
    return (jnp.stack([first_new, second_new]), direction)


def on_device(
    features,
    cotangent,
    counts,
    weights,
    small_params,
    moments_old,
    small_moments,
    basis_attn,
    basis_ffn,
    basis_cols,
):
    groups = MROWS // 8
    gathered = lax.all_gather(weights.astype(bf16), ("dp", "fsdp"), axis=0, tiled=True)
    by_slot = gathered.reshape(groups, 8, D).transpose(1, 0, 2)
    wqkv, wo = by_slot[0:3], by_slot[3]
    wi, wb = by_slot[4:6].reshape(FF, D), by_slot[6:8].reshape(FF, D)
    bias1 = small_params[2 * D : 2 * D + FF].reshape(D, 2).T
    sp = jnp.concatenate(
        [
            small_params[: 2 * D].reshape(2, D),
            bias1,
            small_params[2 * D + FF :].reshape(3, D),
            jnp.zeros((1, D), f32),
        ]
    )
    q, k, v, e, o, li = attn_fwd(features, wqkv)
    output, d1, do, go, gi, gb, gs = rows_pass(counts, features, o, li, cotangent, wo, wi, wb, sp)
    part, gw0 = attn_bwd(0, features, q, k, v, e, o, do, d1, wqkv)
    grad_input, gw1 = attn_bwd(1, features, q, k, v, e, o, do, part, wqkv)
    sum_weights = jnp.stack(
        [
            jnp.concatenate([gw0[0], gw1[0]]),
            jnp.concatenate([gw0[1], gw1[1]]),
            jnp.concatenate([gw0[2], gw1[2]]),
            go,
            gi[:D],
            gi[D:],
            gb[:D],
            gb[D:],
        ],
        axis=1,
    ).reshape(MROWS, D)
    sum_small = jnp.concatenate(
        [gs[0], gs[1], gs[2:4].T.reshape(FF), gs[4], gs[5], gs[6]]
    )
    grad_weights = lax.psum_scatter(sum_weights, ("dp", "fsdp"), scatter_dimension=0, tiled=True)
    grad_small = lax.psum(sum_small, ("dp", "fsdp"))
    count_rows = grad_weights.shape[0]
    row_ids = lax.axis_index(("dp", "fsdp")) * count_rows + jnp.arange(count_rows, dtype=jnp.int32)
    within = row_ids % 8
    group_ids = row_ids // 8
    block_ids = jnp.where(within < 4, within, 4 + (within - 4) // 2)
    inner_ids = jnp.where(within < 4, group_ids, 2 * group_ids + within % 2)
    attn_pick = jnp.minimum(block_ids, 3)
    ffn_pick = jnp.clip(block_ids - 4, 0, 1)
    attn_inner = jnp.minimum(inner_ids, D - 1)
    full_grad = to_plain(
        lax.all_gather(
            grad_weights.astype(jnp.bfloat16), ("dp", "fsdp"), axis=0, tiled=True
        ).astype(grad_weights.dtype)
    )
    left_fwd = row_vectors(
        block_ids, basis_attn[attn_pick, :, attn_inner], basis_ffn[ffn_pick, :, inner_ids]
    )
    rotated = select_right(
        jnp.dot(left_fwd, full_grad, precision=highest), block_ids, basis_cols, False
    )
    moments_new, direction = adam_step(rotated, moments_old)
    full_direction = to_plain(
        lax.all_gather(direction.astype(jnp.bfloat16), ("dp", "fsdp"), axis=0, tiled=True).astype(
            direction.dtype
        )
    )
    left_back = row_vectors(
        block_ids, basis_attn[attn_pick, attn_inner, :], basis_ffn[ffn_pick, inner_ids, :]
    )
    update = select_right(
        jnp.dot(left_back, full_direction, precision=highest), block_ids, basis_cols, True
    )
    weights_new = weights - rate_mats * update
    small_moments_new, small_direction = adam_step(grad_small, small_moments)
    small_new = small_params - rate_small * small_direction
    return (
        output,
        grad_input,
        grad_weights,
        moments_new,
        weights_new,
        grad_small,
        small_moments_new,
        small_new,
    )


def solution(mesh):
    placed = (
        P(("dp", "fsdp"), None, None),
        P(("dp", "fsdp"), None, None),
        P(("dp", "fsdp")),
        P(("dp", "fsdp"), None),
        P(),
        P(None, ("dp", "fsdp"), None),
        P(),
        P(),
        P(),
        P(),
    )
    return jax.shard_map(
        on_device,
        mesh=mesh,
        in_specs=placed,
        out_specs=(
            P(("dp", "fsdp"), None, None),
            P(("dp", "fsdp"), None, None),
            P(("dp", "fsdp"), None),
            P(None, ("dp", "fsdp"), None),
            P(("dp", "fsdp"), None),
            P(),
            P(),
            P(),
        ),
        check_vma=False,
    )
```

time: 945 us -> 598 us (0.63)
  matrix products: 245 us -> 25.7 us
  other arithmetic: 147 us -> 20.9 us
  Pallas kernels: 0 us -> 115 us
  local copies, waits for them, and re-layouts: 198 us -> 112 us
  loops' own time: 32.5 us -> 0 us
    dot_general x50 -> x0, matrix products: 220 us -> none  [the longest x12 37.3 us: times_t(): lax.dot_general(first_mat, second_mat, (((1,), (1,)), ((), ())), preferre...]
    pallas_call x0 -> x4, Pallas kernels: none -> 115 us  [the longest x2 48.7 us: attn_bwd(): pl.pallas_call(attn_bwd_body, grid=(n,), in_specs=[pl.BlockSpec((1, SLOTS...]
    reduce_sum x20 -> x0, other arithmetic: 48.6 us -> none  [the longest x2 18.4 us: hood_forward(): sum_exp = jnp.sum(exponent, axis=-1, keepdims=True)]
    while x238 -> x0, local copies, waits for them, and re-layouts: 32.5 us -> none
    another operation x2 -> x0, loops' own time: 32.5 us -> none  [the longest x1 31.7 us: on_device(): lax.scan(backward_one, initial, (features, live_all, cotangent, kept))]
    add x4 -> x0, other arithmetic: 27.6 us -> none  [backward_one(): return ((totals[0] + grads_w, totals[1] + grads_s), d_rows)]
    convert_element_type x3 -> x1, other arithmetic: 27.3 us -> 1.63 us  [on_device(): weights.astype(bf16)]
    dot_general x6 -> x0, local copies, waits for them, and re-layouts: 15.4 us -> none  [outer_sum(): lax.dot_general(first_mat, second_mat, (((0,), (0,)), ((), ())), preferre...]
  transfers between devices with their start and end apart: 4 -> 4, of which waited for: 4 -> 4; matrix products, arithmetic and copies ran while one was open for 4% -> 6% of each run, Pallas kernels for 0% -> 0%
where the time goes in v1:
time: 598 us; the launch traced here: 589 us
  waiting for transfers between devices  262 us (44%)
  Pallas kernels  115 us (19%)
  local copies, waits for them, and re-layouts  112 us (19%)
  blocking collectives  39.3 us (7%)
  matrix products  25.7 us (4%)
  other arithmetic  20.9 us (3%)
  between operations  14.4 us (2%)
    reduce_scatter x1, waiting for transfers between devices, on_device(): lax.psum_scatter(sum_weights, ('dp', 'fsdp'), scatter_dimension=0, tiled=...  147 us
    all_gather x1, waiting for transfers between devices, on_device(): lax.all_gather(weights.astype(bf16), ('dp', 'fsdp'), axis=0, tiled=True)  64.8 us
    pallas_call x2, Pallas kernels, attn_bwd(): pl.pallas_call(attn_bwd_body, grid=(n,), in_specs=[pl.BlockSpec((1, SLOTS...  48.7 us
    pallas_call x1, Pallas kernels, rows_pass(): pl.pallas_call(rows_body, grid_spec=pltpu.PrefetchScalarGridSpec(num_scal...  41.6 us
    unnamed x57, local copies, waits for them, and re-layouts  40 us
    psum x1, blocking collectives, on_device(): grad_small = lax.psum(sum_small, ('dp', 'fsdp'))  39.3 us
    all_gather x1, waiting for transfers between devices, on_device(): lax.all_gather(grad_weights.astype(jnp.bfloat16), ('dp', 'fsdp'), axis=0,...  30.8 us
    pallas_call x1, Pallas kernels, attn_fwd(): pl.pallas_call(attn_fwd_body, grid=(n, NRB), in_specs=[pl.BlockSpec((1, C...  24.6 us
  transfers between devices with their start and end apart: 4, of which 4 were waited for; matrix products, arithmetic and copies ran while one was open for 6% of the time, Pallas kernels for 0%

profile of v1, /device:TPU:0, one launch (start us, length us, event | category | flops | bytes accessed | tf_op | source)
XLA Modules:
  0.0 589.3 jit_solution(12148047252645020068)
XLA Ops:
  11.4 64.8 %all-gather.4.cloned.1.call-done = bf16[4096,512]{1,0:T(8,128)(2,1)} async-done(((bf16[128,512]{1,0:T(8,128)(2,1)}), bf16[4096,512]{1,0:T(8,128)(2,1)}) %all-gather.4.cloned.1.call-update) | async-done | bytes 4194320 | tf_op jit(solution)/shard_map/all_gather | solution.py:352
  76.2 3.6 copy.45
  83.3 24.6 %attention_forward.1 = (bf16[2,1152,512]{2,1,0:T(8,128)(2,1)}, bf16[2,1024,512]{2,1,0:T(8,128)(2,1)}, bf16[2,1024,512]{2,1,0:T(8,128)(2,1)}, bf16[2,4,1152,1024]...) custom-call(bf16[2,1128,512]{2,1,0:T(8,128)(2,1)} %x_ref.5, bf16[2,1128,512]{2,1,0:T(8,128)(2,1)} %x_ref.5, ...), custom_call_target="tpu_custom_call" | custom-call | flops 14000000000 | bytes 40000000 | tf_op jit(solution)/shard_map/attention_forward/pallas_call | solution.py:75
  107.9 41.6 %rows_forward_backward.1 = (bf16[2,1128,512]{2,1,0:T(8,128)(2,1)}, f32[2,1152,512]{2,1,0:T(8,128)}, bf16[2,1152,512]{2,1,0:T(8,128)(2,1)}, f32[512,512]{1,0:T(8,...) custom-call(s32[2]{0:T(128)} %cnt_ref.1, bf16[2,1128,512]{2,1,0:T(8,128)(2,1)} %x_ref.5, ...), custom_call_target="tpu_custom_call" | custom-call | flops 17999998976 | bytes 30000000 | tf_op jit(solution)/shard_map/rows_forward_backward/pallas_call | solution.py:182
  149.6 18.4 %attention_backward.2 = (f32[2,1128,512]{2,1,0:T(8,128)}, f32[3,256,512]{2,1,0:T(8,128)}) custom-call(bf16[2,1128,512]{2,1,0:T(8,128)(2,1)} %x_ref.5, bf16[2,1152,512]{2,1,0:T(8,128)(2,1)} %get-tuple-element.28.q_ref, bf16[2,1024,512]{2,1,0:T(8,128)(2,1)} %get-tuple-element.29.k_ref, bf16[2,1024,512]{2,1,0:T(8,128)(2,1)} %get-tuple-element.30.v_ref, ...), custom_call_target="tpu_custom_call" | custom-call | flops 8999999488 | bytes 24000000 | tf_op jit(solution)/shard_map/attention_backward/pallas_call | solution.py:252
  168.0 30.3 %attention_backward.3 = (f32[2,1128,512]{2,1,0:T(8,128)}, f32[3,256,512]{2,1,0:T(8,128)}) custom-call(bf16[2,1128,512]{2,1,0:T(8,128)(2,1)} %x_ref.5, bf16[2,1152,512]{2,1,0:T(8,128)(2,1)} %get-tuple-element.28.q_ref, bf16[2,1024,512]{2,1,0:T(8,128)(2,1)} %get-tuple-element.29.k_ref, bf16[2,1024,512]{2,1,0:T(8,128)(2,1)} %get-tuple-element.30.v_ref, ...), custom_call_target="tpu_custom_call" | custom-call | flops 8999999488 | bytes 24000000 | tf_op jit(solution)/shard_map/attention_backward/pallas_call | solution.py:252
  202.7 8.1 %copy.44 = f32[512,8,512]{2,1,0:T(8,128)} copy(f32[512,8,512]{2,0,1:T(8,128)S(1)} %bitcast_dynamic-update-slice_fusion.8) | data formatting | bytes 16777216 | tf_op jit(solution)/shard_map/stack | solution.py:369
  210.9 147.3 %reduce-scatter.2.cloned.1.call-done = f32[128,512]{1,0:T(8,128)} async-done(((f32[4096,512]{1,0:T(8,128)}), f32[128,512]{1,0:T(8,128)}) %reduce-scatter.2.cloned.1.call-update) | async-done | bytes 262160 | tf_op jit(solution)/shard_map/reduce_scatter | solution.py:385
  359.9 5.3 copy.23
  369.4 8.7 %copy.24 = f32[2,1024,1024]{1,2,0:T(8,128)} copy(f32[2,1024,1024]{2,1,0:T(8,128)} %param.18) | data formatting | bytes 16777216 | tf_op args[8]
  388.8 30.8 %all-gather.6.cloned.1.call-done = bf16[4096,512]{1,0:T(8,128)(2,1)} async-done(((bf16[128,512]{1,0:T(8,128)(2,1)}), bf16[4096,512]{1,0:T(8,128)(2,1)}) %all-gather.6.cloned.1.call-update) | async-done | bytes 4194320 | tf_op jit(solution)/shard_map/all_gather | solution.py:397
  426.3 3.9 fusion.35
  430.2 10.1 %fusion.34 = (f32[512,2,512]{2,1,0:T(2,128)}, f32[512,2,512]{2,1,0:T(2,128)}) fusion(f32[512,8,512]{2,1,0:T(8,128)} %copy-done), kind=kLoop, calls=%fused_computation.140 | loop fusion | bytes 8388608 | tf_op jit(solution)/shard_map/slice | solution.py:296
  444.1 3.7 reshape.407
  456.7 8.2 %convolution_bitcast_fusion.1 = f32[128,512,1]{1,0,2:T(8,128)S(1)} fusion(f32[128,4096]{1,0:T(8,128)} %get-tuple-element.77, f32[4096,512]{1,0:T(8,128)} %constant_dynamic-update-slice_fusion), kind=kOutput, calls=%fused_computation.13 | convolution fusion | flops 3221225472 | bytes 10747904 | tf_op jit(solution)/shard_map/dot_general | solution.py:405
  465.0 3.4 fusion.1
  469.8 39.3 %psum.7 = f32[3584]{0:T(1024)S(1)} all-reduce(f32[3584]{0:T(1024)S(1)} %constant_dynamic-update-slice_fusion.5), channel_id=1, replica_groups=mesh['dp'=16,'fsdp'=2] {'dp','fsdp'}, use_global_device_ids=true, to_apply=%region_3.4 | all-reduce | flops 3584 | bytes 28672 | tf_op jit(solution)/shard_map/psum | solution.py:386
  511.4 18.7 %all-gather.8.cloned.1.call-done = bf16[4096,512]{1,0:T(8,128)(2,1)} async-done(((bf16[128,512]{1,0:T(8,128)(2,1)}), bf16[4096,512]{1,0:T(8,128)(2,1)}) %all-gather.8.cloned.1.call-update) | async-done | bytes 4194320 | tf_op jit(solution)/shard_map/all_gather | solution.py:409
  533.6 3.4 copy-done.1
  537.0 3.9 fusion.33
  540.9 10.4 %fusion.32 = (f32[512,2,512]{2,1,0:T(2,128)}, f32[512,2,512]{2,1,0:T(2,128)}) fusion(f32[512,8,512]{2,1,0:T(8,128)} %copy-done.1), kind=kLoop, calls=%fused_computation.138 | loop fusion | bytes 8388608 | tf_op jit(solution)/shard_map/slice | solution.py:296
  555.0 3.7 reshape.411
  567.7 7.5 %convolution_bitcast_fusion = f32[128,512,1]{1,0,2:T(8,128)S(1)} fusion(f32[128,4096]{1,0:T(8,128)} %get-tuple-element.76, f32[4096,512]{1,0:T(8,128)} %constant_dynamic-update-slice_fusion.2), kind=kOutput, calls=%fused_computation.12 | convolution fusion | flops 3221225472 | bytes 10747904 | tf_op jit(solution)/shard_map/dot_general | solution.py:417
  575.3 6.5 %fusion = f32[128,512]{1,0:T(8,128)S(1)} fusion(f32[128,512,1]{1,0,2:T(8,128)S(1)} %convolution_bitcast_fusion, f32[6,512,512]{2,1,0:T(8,128)S(1)} %bitcast.121, f32[6,128]{1,0:T(8,128)S(1)} %fusion.15), kind=kOutput, calls=%fused_computation.9 | convolution fusion | flops 2416640000 | bytes 6818816 | tf_op jit(solution)/shard_map/rk,blk->brl/dot_general | solution.py:321
  (119 shorter events, 68.5 us)
Async XLA Ops:
  7.2 69.0 %all-gather.4.cloned.1.call-start = ((), (), s32[]{:S(2)}) async-start(), calls=%async_computation.1 | async-start | bytes 4325376 | tf_op jit(solution)/shard_map/all_gather | solution.py:352
  8.9 349.4 %reduce-scatter.2.cloned.1.call-start = ((), (), s32[]{:S(2)}) async-start(), calls=%async_computation.2 | async-start | bytes 8650752 | tf_op jit(solution)/shard_map/reduce_scatter | solution.py:385
  168.0 30.3 %copy-start.7 = (f32[3,256,512]{2,1,0:T(8,128)S(1)}, f32[3,256,512]{2,1,0:T(8,128)}, u32[]{:S(2)}) copy-start(f32[3,256,512]{2,1,0:T(8,128)} %get-tuple-element.36) | copy-start | bytes 4718596
  199.9 1.2 copy-start.9
  200.0 1.9 copy-start.6
  200.1 2.4 copy-start.5
  210.9 208.8 %all-gather.6.cloned.1.call-start = ((), (), s32[]{:S(2)}) async-start(), calls=%async_computation.3 | async-start | bytes 4325376 | tf_op jit(solution)/shard_map/all_gather | solution.py:397
  359.9 170.3 %all-gather.8.cloned.1.call-start = ((), (), s32[]{:S(2)}) async-start(), calls=%async_computation.4 | async-start | bytes 4325376 | tf_op jit(solution)/shard_map/all_gather | solution.py:409
  423.0 3.3 copy-start
  450.0 5.1 copy-start.2
  455.1 9.8 %slice-start = ((s8[6291456]{0:T(1024)(128)(4,1)}), s8[4194304]{0:T(1024)(128)(4,1)S(1)}, s32[]{:S(2)}) async-start(s8[6291456]{0:T(1024)(128)(4,1)} %bitcast.118), calls=%async_computation.5 | async-start | bytes 8388608
  456.7 8.3 %slice-start.1 = ((s8[6291456]{0:T(1024)(128)(4,1)}), s8[2097152]{0:T(1024)(128)(4,1)S(1)}, s32[]{:S(2)}) async-start(s8[6291456]{0:T(1024)(128)(4,1)} %bitcast.118), calls=%async_computation.6 | async-start | bytes 4194304
  465.0 3.5 copy-start.4
  465.0 4.3 copy-start.12
  465.0 4.4 copy-start.13
  465.0 44.2 %copy-start.10 = (f32[3584]{0:T(1024)S(1)}, f32[3584]{0:T(1024)}, u32[]{:S(2)}) copy-start(f32[3584]{0:T(1024)} %param.14) | copy-start | bytes 43012
  509.2 24.4 %copy-start.11 = (f32[3584]{0:T(1024)}, f32[3584]{0:T(1024)S(1)}, u32[]{:S(2)}) copy-start(f32[3584]{0:T(1024)S(1)} %psum.7) | copy-start | bytes 43012
  533.6 3.4 copy-start.1
  561.0 5.1 copy-start.3
  564.5 10.7 %slice-start.2 = ((s8[6291456]{0:T(1024)(128)(4,1)}), s8[4194304]{0:T(1024)(128)(4,1)S(1)}, s32[]{:S(2)}) async-start(s8[6291456]{0:T(1024)(128)(4,1)} %bitcast.120), calls=%async_computation.7 | async-start | bytes 8388608
  567.7 7.6 %slice-start.3 = ((s8[6291456]{0:T(1024)(128)(4,1)}), s8[2097152]{0:T(1024)(128)(4,1)S(1)}, s32[]{:S(2)}) async-start(s8[6291456]{0:T(1024)(128)(4,1)} %bitcast.120), calls=%async_computation.8 | async-start | bytes 4194304
  575.2 6.6 %copy-start.8 = (f32[128,512]{1,0:T(8,128)S(1)}, f32[128,512]{1,0:T(8,128)}, u32[]{:S(2)}) copy-start(f32[128,512]{1,0:T(8,128)} %param.13) | copy-start | bytes 786436
Sparse Core Ops, SparseCore 0:
  11.4 64.7 all-gather.3
  211.0 147.1 reduce-scatter.1
  361.7 57.9 all-gather.5
  469.4 60.6 all-gather.7
